TPU v7x, 32 devices: a whole 2x2x4 slice. The times are simulated.
32 devices in a mesh: ctx: 8 (over z, x), head: 4 (over y, core).
Axes of the slice: x: 2, y: 2, z: 4, core: 2. Of those that a mesh axis runs over, the one named last changes fastest.
Arguments:
- hidden: bfloat16 [256, 8192], P(None, 'ctx')
- norm_gain: float32 [8192], replicated, may hold values from 0.1 to 1.9
- w_query: bfloat16 [8192, 8192], P('ctx', 'head'), may hold values from -0.0625 to 0.0625
- manifest_keys: bfloat16 [8, 4096, 128], P(None, 'ctx')
- manifest_values: bfloat16 [8, 4096, 128], P(None, 'ctx'), may hold values from -6 to 6
- w_output: bfloat16 [8192, 8192], P('head', 'ctx'), may hold values from -0.0625 to 0.0625
- valid_len: int32 [256], replicated, may hold values from 1 to 4096, as said below
- home_block: int32 [256], replicated, may hold values from 0 to 7, as said below
Outputs:
- projected: float32 [256, 8192], P('head', 'ctx')
Inputs may be any that keep to these rules, and one draw needn't show every extreme that they name: `valid_len`: every draw has a row that reads the whole manifest and a row with length 1. `home_block`: every draw assigns some row to the first block and some row to the last.
All inputs are finite; a program needn't handle non-finite values.
Results may differ from a plain program's by a relative error of at most 0.005.
The roundings to bfloat16 on the way count: a program that leaves them out, or rounds other values in their place, can miss the bound.
Values may be sent and summed in bfloat16 or wider, within the bound.
A program may use at most 128 MiB of HBM per device.

v0:
```python
import math
import jax
import jax.numpy as jnp
from jax import lax
from jax.sharding import PartitionSpec as P

H = 64
KVH = 8
HD = 128


def shards(
    hidden, norm_gain, w_query, manifest_keys, manifest_values, w_output, valid_len, home_block
):
    ctx_count = lax.axis_size("ctx")
    ctx_index = lax.axis_index("ctx")
    head_index = lax.axis_index("head")
    rows, feat = hidden.shape
    d_model = feat * ctx_count
    width = w_query.shape[1]
    heads_here = width // HD
    group = H // KVH
    span = manifest_keys.shape[1]
    hsplit = min(ctx_count, heads_here)
    rsplit = ctx_count // hsplit
    rows_dev = rows // rsplit
    heads_dev = heads_here // hsplit
    widened = hidden.astype(jnp.float32)
    total_sq = lax.psum(jnp.sum(widened * widened, axis=1, keepdims=True), "ctx")
    inv_rms = lax.rsqrt(total_sq / d_model + 1e-05)
    gain = lax.dynamic_slice_in_dim(norm_gain, ctx_index * feat, feat, 0)
    normed = (widened * inv_rms * gain[None, :]).astype(jnp.bfloat16)
    partial = jnp.dot(normed, w_query, preferred_element_type=jnp.float32)
    partial = partial.reshape(rsplit, rows_dev, hsplit, heads_dev * HD).transpose(2, 0, 1, 3)
    partial = partial.reshape(ctx_count, rows_dev, heads_dev * HD)
    query = lax.psum_scatter(partial, "ctx", scatter_dimension=0, tiled=False).astype(jnp.bfloat16)
    dest_heads = head_index * heads_here + jnp.arange(ctx_count) // rsplit * heads_dev
    dest_kv = dest_heads // group
    kv = jnp.stack([manifest_keys[dest_kv], manifest_values[dest_kv]], axis=1)
    kv = lax.all_to_all(kv, "ctx", split_axis=0, concat_axis=0, tiled=True)
    kv = kv.transpose(1, 0, 2, 3).reshape(2, ctx_count * span, HD)
    keys, values = (kv[0], kv[1])
    first_row = ctx_index % rsplit * rows_dev
    lens = lax.dynamic_slice_in_dim(valid_len, first_row, rows_dev, 0)
    blocks = lax.dynamic_slice_in_dim(home_block, first_row, rows_dev, 0)
    places = jnp.arange(ctx_count * span, dtype=jnp.int32)
    usable = (places[None, :] < lens[:, None]) | ((places // span)[None, :] == blocks[:, None])
    usable = usable[:, None, :]
    q3 = query.reshape(rows_dev, heads_dev, HD)
    scores = jnp.einsum("nhd,jd->nhj", q3, keys, preferred_element_type=jnp.float32) * (
        1.0 / math.sqrt(HD)
    )
    scores = jnp.where(usable, scores, -1e30)
    row_max = jnp.max(scores, axis=2, keepdims=True)
    expo = jnp.where(usable, jnp.exp(scores - row_max), 0.0)
    row_sum = jnp.sum(expo, axis=2, keepdims=True)
    weighted = jnp.einsum(
        "nhj,jd->nhd", expo.astype(jnp.bfloat16), values, preferred_element_type=jnp.float32
    )
    attn = (weighted / row_sum).astype(jnp.bfloat16).reshape(rows_dev, heads_dev * HD)
    attn = lax.all_gather(attn, "ctx", axis=0, tiled=False)
    attn = attn.reshape(hsplit, rsplit, rows_dev, heads_dev * HD).transpose(1, 2, 0, 3)
    attn = attn.reshape(rows, width)
    return lax.psum_scatter(
        jnp.dot(attn, w_output, preferred_element_type=jnp.float32),
        "head",
        scatter_dimension=0,
        tiled=True,
    )


def solution(mesh):
    in_specs = (
        P(None, "ctx"),
        P(),
        P("ctx", "head"),
        P(None, "ctx", None),
        P(None, "ctx", None),
        P("head", "ctx"),
        P(),
        P(),
    )
    out_specs = P("head", "ctx")
    return jax.shard_map(shards, mesh=mesh, in_specs=in_specs, out_specs=out_specs, check_vma=False)
```

profile of v0, /device:TPU:0, one launch (start us, length us, event | category | flops | bytes accessed | tf_op | source)
XLA Modules:
  0.0 222.7 jit_solution(15778530597544170264)
XLA Ops:
  6.5 0.0 copy-start
  6.5 0.0 reduce-scatter.3.cloned.1.call-start
  6.5 1.3 fusion.14
  7.9 23.1 %psum.7 = f32[256,1]{0,1:T(1,128)S(1)} all-reduce(f32[256,1]{0,1:T(1,128)S(1)} %bitcast.42), channel_id=1, replica_groups=mesh['ctx'=8,'head'=4] {'ctx'}, use_global_device_ids=true, to_apply=%region_1.0 | all-reduce | flops 256 | bytes 2048 | tf_op jit(solution)/shard_map/psum | solution.py:29
  31.0 0.7 dynamic_slice.2
  31.6 5.5 %fusion.19 = f32[256,2048]{0,1:T(8,128)} fusion(bf16[1024,2048]{1,0:T(8,128)(2,1)} %param.10, bf16[256,1024]{1,0:T(8,128)(2,1)} %param.8, f32[1024]{0:T(1024)S(1)} %dynamic_slice.2, f32[256]{0:T(256)S(1)} %bitcast.43), kind=kOutput, calls=%fused_computation.22 | convolution fusion | flops 1074790400 | bytes 6820864 | tf_op jit(solution)/shard_map/reshape | solution.py:34
  37.2 0.0 reduce-scatter.3.cloned.1.call-update
  37.2 0.0 copy-done
  37.2 0.7 gather_fusion.1
  38.0 2.0 gather_fusion
  40.0 0.0 copy-start.2
  40.0 0.0 copy-start.3
  40.0 1.5 pad_maximum_fusion
  41.5 3.6 %all-to-all-start = ((bf16[8,2,512,128]{3,2,1,0:T(8,128)(2,1)}), bf16[8,2,512,128]{3,2,1,0:T(8,128)(2,1)S(1)}, u32[]{:S(2)}, u32[]{:S(2)}) async-start(bf16[8,2,512,128]{3,2,1,0:T(8,128)(2,1)} %pad_maximum_fusion), calls=%async_computation.1 | async-start | bytes 4194304 | tf_op jit(solution)/shard_map/all_to_all | solution.py:40
  45.1 0.0 all-gather.2.cloned.1.call-start
  45.1 0.0 copy-done.2
  45.2 0.0 copy-done.3
  45.2 1.9 fusion.6
  47.0 59.5 %all-to-all-done = bf16[8,2,512,128]{3,2,1,0:T(8,128)(2,1)S(1)} async-done(((bf16[8,2,512,128]{3,2,1,0:T(8,128)(2,1)}), bf16[8,2,512,128]{3,2,1,0:T(8,128)(2,1)S(1)}, u32[]{:S(2)}, u32[]{:S(2)}) %all-to-all-start) | async-done | bytes 2097184 | tf_op jit(solution)/shard_map/all_to_all | solution.py:40
  106.5 1.5 fusion.29
  108.0 25.2 %reduce-scatter.3.cloned.1.call-done = f32[1,256,256]{1,2,0:T(8,128)} async-done(((f32[8,256,256]{1,2,0:T(8,128)}), f32[1,256,256]{1,2,0:T(8,128)}) %reduce-scatter.3.cloned.1.call-update) | async-done | bytes 262160 | tf_op jit(solution)/shard_map/reduce_scatter | solution.py:36
  133.2 1.0 convert_element_type.21
  134.2 0.0 copy-start.1
  134.2 8.3 %fusion.30 = (f32[256,2]{0,1:T(2,128)S(1)}, bf16[256,2,4096]{2,0,1:T(8,128)(2,1)}) fusion(pred[256,4096]{1,0:T(8,128)(4,1)} %fusion.6, bf16[256,2,128]{0,2,1:T(8,128)(2,1)S(1)} %bitcast.41, bf16[4096,128,1]{1,0,2:T(8,128)(2,1)} %bitcast.39), kind=kOutput, calls=%fused_computation.43 | convolution fusion | flops 549457920 | bytes 6424576 | tf_op jit(solution)/shard_map/sub | solution.py:55
  142.5 0.0 copy-done.1
  142.5 3.7 %fusion.11 = bf16[256,2,128]{0,2,1:T(8,128)(2,1)S(1)} fusion(bf16[4096,128,1]{1,0,2:T(8,128)(2,1)S(1)} %bitcast.34, bf16[256,2,4096]{2,0,1:T(8,128)(2,1)} %get-tuple-element.8, f32[256,2]{0,1:T(2,128)S(1)} %get-tuple-element.7), kind=kOutput, calls=%fused_computation.17 | convolution fusion | flops 537001984 | bytes 5376000 | tf_op jit(solution)/shard_map/nhj,jd->nhd/dot_general | solution.py:57
  146.2 0.8 copy.20
  146.9 0.0 all-gather.2.cloned.1.call-update
  147.0 0.0 reduce-scatter.5.cloned.1.call-start
  147.0 39.4 %all-gather.2.cloned.1.call-done = bf16[8,256,256]{2,1,0:T(8,128)(2,1)} async-done(((bf16[1,256,256]{2,1,0:T(8,128)(2,1)}), bf16[8,256,256]{2,1,0:T(8,128)(2,1)}) %all-gather.2.cloned.1.call-update) | async-done | bytes 1048592 | tf_op jit(solution)/shard_map/all_gather | solution.py:61
  186.4 1.5 copy.21
  187.9 4.5 %fusion.31 = f32[256,1024]{1,0:T(8,128)} fusion(bf16[256,2048]{0,1:T(8,128)(2,1)S(1)} %bitcast.38, bf16[2048,1024]{1,0:T(8,128)(2,1)} %param.13), kind=kOutput, calls=%fused_computation.44 | convolution fusion | flops 1073741824 | bytes 6291456 | tf_op jit(solution)/shard_map/dot_general | solution.py:65
  192.4 0.0 reduce-scatter.5.cloned.1.call-update
  192.4 23.8 %reduce-scatter.5.cloned.1.call-done = f32[64,1024]{1,0:T(8,128)} async-done(((f32[256,1024]{1,0:T(8,128)}), f32[64,1024]{1,0:T(8,128)}) %reduce-scatter.5.cloned.1.call-update) | async-done | bytes 262160 | tf_op jit(solution)/shard_map/reduce_scatter | solution.py:64
  (4 shorter events, 0.0 us)
Async XLA Ops:
  6.5 30.7 %copy-start = (bf16[8,512,128]{2,1,0:T(8,128)(2,1)S(1)}, bf16[8,512,128]{2,1,0:T(8,128)(2,1)}, u32[]{:S(2)}) copy-start(bf16[8,512,128]{2,1,0:T(8,128)(2,1)} %param.12) | copy-start | bytes 3145732
  6.5 126.7 %reduce-scatter.3.cloned.1.call-start = ((), (), s32[]{:S(2)}) async-start(), calls=%async_computation.3 | async-start | bytes 2359296 | tf_op jit(solution)/shard_map/reduce_scatter | solution.py:36
  40.0 5.2 %copy-start.2 = (s32[256]{0:T(256)S(1)}, s32[256]{0:T(256)}, u32[]{:S(2)}) copy-start(s32[256]{0:T(256)} %param.14) | copy-start | bytes 3076
  40.0 5.2 %copy-start.3 = (s32[256]{0:T(256)S(1)}, s32[256]{0:T(256)}, u32[]{:S(2)}) copy-start(s32[256]{0:T(256)} %param.15) | copy-start | bytes 3076
  41.5 65.0 %all-to-all-start = ((bf16[8,2,512,128]{3,2,1,0:T(8,128)(2,1)}), bf16[8,2,512,128]{3,2,1,0:T(8,128)(2,1)S(1)}, u32[]{:S(2)}, u32[]{:S(2)}) async-start(bf16[8,2,512,128]{3,2,1,0:T(8,128)(2,1)} %pad_maximum_fusion), calls=%async_computation.1 | async-start | bytes 4194304 | tf_op jit(solution)/shard_map/all_to_all | solution.py:40
  45.1 141.3 %all-gather.2.cloned.1.call-start = ((), (), s32[]{:S(2)}) async-start(), calls=%async_computation.4 | async-start | bytes 1179648 | tf_op jit(solution)/shard_map/all_gather | solution.py:61
  134.2 8.3 %copy-start.1 = (bf16[1,8,512,128]{3,2,0,1:T(8,128)(2,1)S(1)}, bf16[1,8,512,128]{3,2,0,1:T(8,128)(2,1)}, u32[]{:S(2)}) copy-start(bf16[1,8,512,128]{3,2,0,1:T(8,128)(2,1)} %get-tuple-element.6) | copy-start | bytes 3145732
  147.0 69.2 %reduce-scatter.5.cloned.1.call-start = ((), (), s32[]{:S(2)}) async-start(), calls=%async_computation.5 | async-start | bytes 1310720 | tf_op jit(solution)/shard_map/reduce_scatter | solution.py:64
Sparse Core Ops, SparseCore 0:
  37.3 95.8 reduce-scatter.2
  147.1 39.2 all-gather.1
  192.5 23.6 reduce-scatter.4
where the time goes:
time: 223 us
  waiting for transfers between devices  148 us (66%)
  blocking collectives  23.1 us (10%)
  matrix products  22 us (10%)
  between operations  13.2 us (6%)
  local copies, waits for them, and re-layouts  7.19 us (3%)
  other arithmetic  5.66 us (3%)
  starting transfers between devices  3.69 us (2%)
    all_to_all x1, waiting for transfers between devices, shards(): kv = lax.all_to_all(kv, 'ctx', split_axis=0, concat_axis=0, tiled=True)  59.5 us
    all_gather x1, waiting for transfers between devices, shards(): attn = lax.all_gather(attn, 'ctx', axis=0, tiled=False)  39.4 us
    reduce_scatter x1, waiting for transfers between devices, shards(): lax.psum_scatter(partial, 'ctx', scatter_dimension=0, tiled=False)  25.2 us
    reduce_scatter x1, waiting for transfers between devices, shards(): lax.psum_scatter(jnp.dot(attn, w_output, preferred_element_type=jnp.float...  23.8 us
    psum x1, blocking collectives, shards(): lax.psum(jnp.sum(widened * widened, axis=1, keepdims=True), 'ctx')  23.1 us
    sub x1, matrix products, shards(): expo = jnp.where(usable, jnp.exp(scores - row_max), 0.0)  8.3 us
    reshape x1, matrix products, shards(): partial.reshape(rsplit, rows_dev, hsplit, heads_dev * HD)  5.51 us
    dot_general x1, matrix products, shards(): jnp.dot(attn, w_output, preferred_element_type=jnp.float32)  4.46 us
  transfers between devices with their start and end apart: 4, of which 4 were waited for; matrix products, arithmetic and copies ran while one was open for 3% of the time, Pallas kernels for 0%

commit v1 on v0

--- a/solution.py
+++ b/solution.py
@@ -7,6 +7,18 @@
 H = 64
 KVH = 8
 HD = 128
+
+
+def in_blocks(x, dim, length):
+    dims = x.shape
+    blocks = x.reshape(*dims[:dim], length, dims[dim] // length, *dims[dim + 1 :])
+    return jnp.moveaxis(blocks, dim, 0)
+
+
+def in_order(tiles, dim):
+    tiles = jnp.moveaxis(tiles, 0, dim)
+    shape = tiles.shape
+    return tiles.reshape(*shape[:dim], shape[dim] * shape[dim + 1], *shape[dim + 2 :])
 
 
 def shards(
@@ -37,7 +49,14 @@
     dest_heads = head_index * heads_here + jnp.arange(ctx_count) // rsplit * heads_dev
     dest_kv = dest_heads // group
     kv = jnp.stack([manifest_keys[dest_kv], manifest_values[dest_kv]], axis=1)
-    kv = lax.all_to_all(kv, "ctx", split_axis=0, concat_axis=0, tiled=True)
+    peers, index = (lax.axis_size("ctx"), lax.axis_index("ctx"))
+    pieces = in_blocks(kv, 0, peers)
+    outs = [pieces[index]]
+    for step in range(1, peers):
+        sent = pieces[index ^ step]
+        outs.append(lax.ppermute(sent, "ctx", [(i, i ^ step) for i in range(peers)]))
+    pieces = jnp.stack(outs)[index ^ jnp.arange(peers)]
+    kv = in_order(pieces, 0)
     kv = kv.transpose(1, 0, 2, 3).reshape(2, ctx_count * span, HD)
     keys, values = (kv[0], kv[1])
     first_row = ctx_index % rsplit * rows_dev

time: 223 us -> 216 us (0.969)
  waiting for transfers between devices: 148 us -> 129 us
  local copies, waits for them, and re-layouts: 7.19 us -> 16 us
  starting transfers between devices: 3.69 us -> 6.85 us
    all_to_all x1 -> x0, waiting for transfers between devices: 59.5 us -> none  [shards(): kv = lax.all_to_all(kv, 'ctx', split_axis=0, concat_axis=0, tiled=True)]
    ppermute x0 -> x7, waiting for transfers between devices: none -> 44.2 us  [shards(): lax.ppermute(sent, 'ctx', [(i, i ^ step) for i in range(peers)])]
    ppermute x0 -> x7, starting transfers between devices: none -> 6.77 us  [shards(): lax.ppermute(sent, 'ctx', [(i, i ^ step) for i in range(peers)])]
    unnamed x8 -> x20, local copies, waits for them, and re-layouts: 0.02 us -> 5.34 us
    reduce_scatter x1, waiting for transfers between devices: 25.2 us -> 21.3 us  [shards(): lax.psum_scatter(partial, 'ctx', scatter_dimension=0, tiled=False)]
    all_to_all x1 -> x0, starting transfers between devices: 3.6 us -> none  [shards(): kv = lax.all_to_all(kv, 'ctx', split_axis=0, concat_axis=0, tiled=True)]
    gather x0 -> x1, local copies, waits for them, and re-layouts: none -> 2.55 us  [shards(): pieces = jnp.stack(outs)[index ^ jnp.arange(peers)]]
  transfers between devices with their start and end apart: 4 -> 10, of which waited for: 4 -> 8; matrix products, arithmetic and copies ran while one was open for 3% -> 7% of each run, Pallas kernels for 0% -> 0%
where the time goes in v1:
time: 216 us; the launch traced here: 215 us
  waiting for transfers between devices  129 us (60%)
  blocking collectives  23.1 us (11%)
  matrix products  21.9 us (10%)
  local copies, waits for them, and re-layouts  16 us (7%)
  between operations  13.3 us (6%)
  starting transfers between devices  6.85 us (3%)
  other arithmetic  5.41 us (3%)
    ppermute x7, waiting for transfers between devices, shards(): lax.ppermute(sent, 'ctx', [(i, i ^ step) for i in range(peers)])  44.2 us
    all_gather x1, waiting for transfers between devices, shards(): attn = lax.all_gather(attn, 'ctx', axis=0, tiled=False)  39.4 us
    reduce_scatter x1, waiting for transfers between devices, shards(): lax.psum_scatter(jnp.dot(attn, w_output, preferred_element_type=jnp.float...  23.8 us
    psum x1, blocking collectives, shards(): lax.psum(jnp.sum(widened * widened, axis=1, keepdims=True), 'ctx')  23.1 us
    reduce_scatter x1, waiting for transfers between devices, shards(): lax.psum_scatter(partial, 'ctx', scatter_dimension=0, tiled=False)  21.3 us
    sub x1, matrix products, shards(): expo = jnp.where(usable, jnp.exp(scores - row_max), 0.0)  8.31 us
    ppermute x7, starting transfers between devices, shards(): lax.ppermute(sent, 'ctx', [(i, i ^ step) for i in range(peers)])  6.77 us
    reshape x1, matrix products, shards(): partial.reshape(rsplit, rows_dev, hsplit, heads_dev * HD)  5.5 us
  transfers between devices with their start and end apart: 10, of which 8 were waited for; matrix products, arithmetic and copies ran while one was open for 7% of the time, Pallas kernels for 0%

profile of v1, /device:TPU:0, one launch (start us, length us, event | category | flops | bytes accessed | tf_op | source)
XLA Modules:
  0.0 215.4 jit_solution(11695583335263270909)
XLA Ops:
  6.5 1.3 fusion.14
  7.9 23.1 %psum.7 = f32[256,1]{0,1:T(1,128)S(1)} all-reduce(f32[256,1]{0,1:T(1,128)S(1)} %bitcast.78), channel_id=1, replica_groups=mesh['ctx'=8,'head'=4] {'ctx'}, use_global_device_ids=true, to_apply=%region_1.0 | all-reduce | flops 256 | bytes 2048 | tf_op jit(solution)/shard_map/psum | solution.py:41
  31.0 0.7 dynamic_slice.4
  31.6 5.5 %fusion.19 = f32[256,2048]{0,1:T(8,128)} fusion(bf16[1024,2048]{1,0:T(8,128)(2,1)} %param.10, bf16[256,1024]{1,0:T(8,128)(2,1)} %param.8, f32[1024]{0:T(1024)S(1)} %dynamic_slice.4, f32[256]{0:T(256)S(1)} %bitcast.79), kind=kOutput, calls=%fused_computation.38 | convolution fusion | flops 1074790400 | bytes 6820864 | tf_op jit(solution)/shard_map/reshape | solution.py:46
  37.2 0.0 reduce-scatter.3.cloned.1.call-update
  37.2 0.0 all-gather.2.cloned.1.call-start
  37.3 0.7 gather_fusion.1
  38.0 2.0 gather_fusion
  40.1 0.0 copy-start.5
  40.1 0.0 copy-start.6
  40.1 0.1 collective-permute-start.5
  40.2 1.2 fusion.23
  41.4 1.0 collective-permute-start.6
  42.4 4.2 %collective-permute-start = (bf16[1,2,512,128]{3,2,1,0:T(8,128)(2,1)}, bf16[1,2,512,128]{3,2,1,0:T(8,128)(2,1)}, u32[]{:S(2)}, u32[]{:S(2)}) collective-permute-start(bf16[1,2,512,128]{3,2,1,0:T(8,128)(2,1)} %get-tuple-element.8), channel_id=1, source_target_pairs={{0,4},{4,0},{8,12},{12,8},{16,20},{20,16},{24,28},{28,24},{1,5},{5... | collective-permute-start | bytes 786440 | tf_op jit(solution)/shard_map/ppermute | solution.py:57
  46.6 0.0 collective-permute-start.1
  46.6 1.5 collective-permute-start.2
  48.1 0.0 copy-done.5
  48.1 1.9 fusion.6
  50.0 6.9 %collective-permute-done = bf16[1,2,512,128]{3,2,1,0:T(8,128)(2,1)} collective-permute-done((bf16[1,2,512,128]{3,2,1,0:T(8,128)(2,1)}, bf16[1,2,512,128]{3,2,1,0:T(8,128)(2,1)}, u32[]{:S(2)}, u32[]{:S(2)}) %collective-permute-start) | collective-permute-done | bytes 262176 | tf_op jit(solution)/shard_map/ppermute | solution.py:57
  57.0 0.0 collective-permute-start.3
  57.0 1.0 bitcast_dynamic-update-slice_fusion.6
  57.9 16.1 %collective-permute-done.1 = bf16[1,2,512,128]{3,2,1,0:T(8,128)(2,1)} collective-permute-done((bf16[1,2,512,128]{3,2,1,0:T(8,128)(2,1)}, bf16[1,2,512,128]{3,2,1,0:T(8,128)(2,1)}, u32[]{:S(2)}, u32[]{:S(2)}) %collective-permute-start.1) | collective-permute-done | bytes 262176 | tf_op jit(solution)/shard_map/ppermute | solution.py:57
  74.0 0.0 collective-permute-start.4
  74.0 1.0 bitcast_dynamic-update-slice_fusion.5
  75.0 9.3 %collective-permute-done.2 = bf16[1,2,512,128]{3,2,1,0:T(8,128)(2,1)} collective-permute-done((bf16[1,2,512,128]{3,2,1,0:T(8,128)(2,1)}, bf16[1,2,512,128]{3,2,1,0:T(8,128)(2,1)}, u32[]{:S(2)}, u32[]{:S(2)}) %collective-permute-start.2) | collective-permute-done | bytes 262176 | tf_op jit(solution)/shard_map/ppermute | solution.py:57
  84.3 1.0 bitcast_dynamic-update-slice_fusion.4
  85.3 10.9 %collective-permute-done.3 = bf16[1,2,512,128]{3,2,1,0:T(8,128)(2,1)S(1)} collective-permute-done((bf16[1,2,512,128]{3,2,1,0:T(8,128)(2,1)S(1)}, bf16[1,2,512,128]{3,2,1,0:T(8,128)(2,1)S(1)}, u32[]{:S(2)}, u32[]{:S(2)}) %collective-permute-start.3) | collective-permute-done | bytes 262176 | tf_op jit(solution)/shard_map/ppermute | solution.py:57
  96.2 1.0 collective-permute-done.4
  97.2 0.0 collective-permute-done.5
  97.3 1.0 bitcast_dynamic-update-slice_fusion.1
  98.2 0.0 collective-permute-done.6
  98.3 1.0 bitcast_dynamic-update-slice_fusion
  99.3 1.3 copy-done.2
  100.6 2.5 %gather_fusion.2 = bf16[8,2,512,128]{3,2,1,0:T(8,128)(2,1)S(1)} fusion(bf16[8,2,512,128]{3,2,1,0:T(8,128)(2,1)} %bitcast.72, s32[1024]{0:T(1024)S(1)} %pad_clamp_fusion), kind=kCustom, calls=%fused_computation.2 | custom fusion | bytes 4194336 | tf_op jit(solution)/shard_map/gather | solution.py:58
  103.1 1.5 fusion.44
  104.6 21.3 %reduce-scatter.3.cloned.1.call-done = f32[1,256,256]{1,2,0:T(8,128)} async-done(((f32[8,256,256]{1,2,0:T(8,128)}), f32[1,256,256]{1,2,0:T(8,128)}) %reduce-scatter.3.cloned.1.call-update) | async-done | bytes 262160 | tf_op jit(solution)/shard_map/reduce_scatter | solution.py:48
  125.9 1.0 convert_element_type.21
  126.9 0.0 copy-start.1
  126.9 8.3 %fusion.45 = (f32[256,2]{0,1:T(2,128)S(1)}, bf16[256,2,4096]{2,0,1:T(8,128)(2,1)}) fusion(pred[256,4096]{1,0:T(8,128)(4,1)} %fusion.6, bf16[256,2,128]{0,2,1:T(8,128)(2,1)S(1)} %bitcast.77, bf16[4096,128,1]{1,0,2:T(8,128)(2,1)} %bitcast.75), kind=kOutput, calls=%fused_computation.84 | convolution fusion | flops 549457920 | bytes 6424576 | tf_op jit(solution)/shard_map/sub | solution.py:74
  135.2 3.7 %fusion.11 = bf16[256,2,128]{0,2,1:T(8,128)(2,1)S(1)} fusion(bf16[4096,128,1]{1,0,2:T(8,128)(2,1)S(1)} %bitcast.71, bf16[256,2,4096]{2,0,1:T(8,128)(2,1)} %get-tuple-element.14, f32[256,2]{0,1:T(2,128)S(1)} %get-tuple-element.13), kind=kOutput, calls=%fused_computation.33 | convolution fusion | flops 537001984 | bytes 5376000 | tf_op jit(solution)/shard_map/nhj,jd->nhd/dot_general | solution.py:76
  138.9 0.8 copy.44
  139.7 0.0 all-gather.2.cloned.1.call-update
  139.7 0.0 reduce-scatter.5.cloned.1.call-start
  139.7 39.4 %all-gather.2.cloned.1.call-done = bf16[8,256,256]{2,1,0:T(8,128)(2,1)} async-done(((bf16[1,256,256]{2,1,0:T(8,128)(2,1)}), bf16[8,256,256]{2,1,0:T(8,128)(2,1)}) %all-gather.2.cloned.1.call-update) | async-done | bytes 1048592 | tf_op jit(solution)/shard_map/all_gather | solution.py:80
  179.1 1.5 copy.45
  180.6 4.4 %fusion.46 = f32[256,1024]{1,0:T(8,128)} fusion(bf16[256,2048]{0,1:T(8,128)(2,1)S(1)} %bitcast.74, bf16[2048,1024]{1,0:T(8,128)(2,1)} %param.13), kind=kOutput, calls=%fused_computation.85 | convolution fusion | flops 1073741824 | bytes 6291456 | tf_op jit(solution)/shard_map/dot_general | solution.py:84
  185.0 0.0 reduce-scatter.5.cloned.1.call-update
  185.0 23.8 %reduce-scatter.5.cloned.1.call-done = f32[64,1024]{1,0:T(8,128)} async-done(((f32[256,1024]{1,0:T(8,128)}), f32[64,1024]{1,0:T(8,128)}) %reduce-scatter.5.cloned.1.call-update) | async-done | bytes 262160 | tf_op jit(solution)/shard_map/reduce_scatter | solution.py:83
  (20 shorter events, 0.2 us)
Async XLA Ops:
  6.5 30.7 %copy-start = (bf16[8,512,128]{2,1,0:T(8,128)(2,1)S(1)}, bf16[8,512,128]{2,1,0:T(8,128)(2,1)}, u32[]{:S(2)}) copy-start(bf16[8,512,128]{2,1,0:T(8,128)(2,1)} %param.12) | copy-start | bytes 3145732
  6.5 119.4 %reduce-scatter.3.cloned.1.call-start = ((), (), s32[]{:S(2)}) async-start(), calls=%async_computation.2 | async-start | bytes 2359296 | tf_op jit(solution)/shard_map/reduce_scatter | solution.py:48
  37.2 141.9 %all-gather.2.cloned.1.call-start = ((), (), s32[]{:S(2)}) async-start(), calls=%async_computation.3 | async-start | bytes 1179648 | tf_op jit(solution)/shard_map/all_gather | solution.py:80
  40.1 8.0 %copy-start.5 = (s32[256]{0:T(256)S(1)}, s32[256]{0:T(256)}, u32[]{:S(2)}) copy-start(s32[256]{0:T(256)} %param.14) | copy-start | bytes 3076
  40.1 8.0 %copy-start.6 = (s32[256]{0:T(256)S(1)}, s32[256]{0:T(256)}, u32[]{:S(2)}) copy-start(s32[256]{0:T(256)} %param.15) | copy-start | bytes 3076
  40.1 57.2 %collective-permute-start.5 = (bf16[1,2,512,128]{3,2,1,0:T(8,128)(2,1)S(1)}, bf16[1,2,512,128]{3,2,1,0:T(8,128)(2,1)}, u32[]{:S(2)}, u32[]{:S(2)}) collective-permute-start(bf16[1,2,512,128]{3,2,1,0:T(8,128)(2,1)S(1)} %fusion.31), channel_id=1, source_target_pairs={{0,24},{4,28},{8,16},{12,20},{16,8},{20,12},{24,0},{28,4},{1,25},{... | collective-permute-start | bytes 786440 | tf_op jit(solution)/shard_map/ppermute | solution.py:57
  41.4 56.9 %collective-permute-start.6 = (bf16[1,2,512,128]{3,2,0,1:T(8,128)(2,1)}, bf16[1,2,512,128]{3,2,0,1:T(8,128)(2,1)}, u32[]{:S(2)}, u32[]{:S(2)}) collective-permute-start(bf16[1,2,512,128]{3,2,0,1:T(8,128)(2,1)} %get-tuple-element.7), channel_id=1, source_target_pairs={{0,28},{4,24},{8,20},{12,16},{16,12},{20,8},{24,4},{28,0},{1,29},{... | collective-permute-start | bytes 786440 | tf_op jit(solution)/shard_map/ppermute | solution.py:57
  42.4 14.5 %collective-permute-start = (bf16[1,2,512,128]{3,2,1,0:T(8,128)(2,1)}, bf16[1,2,512,128]{3,2,1,0:T(8,128)(2,1)}, u32[]{:S(2)}, u32[]{:S(2)}) collective-permute-start(bf16[1,2,512,128]{3,2,1,0:T(8,128)(2,1)} %get-tuple-element.8), channel_id=1, source_target_pairs={{0,4},{4,0},{8,12},{12,8},{16,20},{20,16},{24,28},{28,24},{1,5},{5... | collective-permute-start | bytes 786440 | tf_op jit(solution)/shard_map/ppermute | solution.py:57
  46.6 27.4 %collective-permute-start.1 = (bf16[1,2,512,128]{3,2,1,0:T(8,128)(2,1)}, bf16[1,2,512,128]{3,2,1,0:T(8,128)(2,1)}, u32[]{:S(2)}, u32[]{:S(2)}) collective-permute-start(bf16[1,2,512,128]{3,2,1,0:T(8,128)(2,1)} %get-tuple-element.9), channel_id=1, source_target_pairs={{0,8},{4,12},{8,0},{12,4},{16,24},{20,28},{24,16},{28,20},{1,9},{5... | collective-permute-start | bytes 786440 | tf_op jit(solution)/shard_map/ppermute | solution.py:57
  46.6 37.7 %collective-permute-start.2 = (bf16[1,2,512,128]{3,2,1,0:T(8,128)(2,1)}, bf16[1,2,512,128]{3,2,1,0:T(8,128)(2,1)}, u32[]{:S(2)}, u32[]{:S(2)}) collective-permute-start(bf16[1,2,512,128]{3,2,1,0:T(8,128)(2,1)} %get-tuple-element.10), channel_id=1, source_target_pairs={{0,12},{4,8},{8,4},{12,0},{16,28},{20,24},{24,20},{28,16},{1,13},{... | collective-permute-start | bytes 786440 | tf_op jit(solution)/shard_map/ppermute | solution.py:57
  50.0 7.0 %copy-start.4 = (bf16[1,2,512,128]{3,2,1,0:T(8,128)(2,1)S(1)}, bf16[1,2,512,128]{3,2,1,0:T(8,128)(2,1)}, u32[]{:S(2)}) copy-start(bf16[1,2,512,128]{3,2,1,0:T(8,128)(2,1)} %get-tuple-element.11) | copy-start | bytes 786436
  50.0 24.1 %copy-start.3 = (bf16[1,2,512,128]{3,2,1,0:T(8,128)(2,1)S(1)}, bf16[1,2,512,128]{3,2,1,0:T(8,128)(2,1)}, u32[]{:S(2)}) copy-start(bf16[1,2,512,128]{3,2,1,0:T(8,128)(2,1)} %get-tuple-element.12) | copy-start | bytes 786436
  57.0 39.2 %collective-permute-start.3 = (bf16[1,2,512,128]{3,2,1,0:T(8,128)(2,1)S(1)}, bf16[1,2,512,128]{3,2,1,0:T(8,128)(2,1)S(1)}, u32[]{:S(2)}, u32[]{:S(2)}) collective-permute-start(bf16[1,2,512,128]{3,2,1,0:T(8,128)(2,1)S(1)} %copy-done.4), channel_id=1, source_target_pairs={{0,16},{4,20},{8,24},{12,28},{16,0},{20,4},{24,8},{28,12},{1,17},{... | collective-permute-start | bytes 786440 | tf_op jit(solution)/shard_map/ppermute | solution.py:57
  74.0 23.2 %collective-permute-start.4 = (bf16[1,2,512,128]{3,2,1,0:T(8,128)(2,1)S(1)}, bf16[1,2,512,128]{3,2,1,0:T(8,128)(2,1)S(1)}, u32[]{:S(2)}, u32[]{:S(2)}) collective-permute-start(bf16[1,2,512,128]{3,2,1,0:T(8,128)(2,1)S(1)} %copy-done.3), channel_id=1, source_target_pairs={{0,20},{4,16},{8,28},{12,24},{16,4},{20,0},{24,12},{28,8},{1,21},{... | collective-permute-start | bytes 786440 | tf_op jit(solution)/shard_map/ppermute | solution.py:57
  99.2 1.3 copy-start.2
  126.9 8.3 %copy-start.1 = (bf16[1,8,512,128]{3,2,0,1:T(8,128)(2,1)S(1)}, bf16[1,8,512,128]{3,2,0,1:T(8,128)(2,1)}, u32[]{:S(2)}) copy-start(bf16[1,8,512,128]{3,2,0,1:T(8,128)(2,1)} %get-tuple-element.6) | copy-start | bytes 3145732
  139.7 69.2 %reduce-scatter.5.cloned.1.call-start = ((), (), s32[]{:S(2)}) async-start(), calls=%async_computation.4 | async-start | bytes 1310720 | tf_op jit(solution)/shard_map/reduce_scatter | solution.py:83
Sparse Core Ops, SparseCore 0:
  37.3 88.5 reduce-scatter.2
  139.8 39.2 all-gather.1
  185.2 23.6 reduce-scatter.4
